TPU v7x, 256 devices: a whole 4x4x8 slice. The times are simulated.
256 devices in a mesh: seq: 32 (over x_lo, z, core), chan: 8 (over x_hi, y).
Axes of the slice: x: 4 (x_hi: 2, x_lo: 2; x = x_hi * 2 + x_lo), y: 4, z: 8, core: 2. Of those that a mesh axis runs over, the one named last changes fastest.
Arguments:
- inputs: bfloat16 [262144, 1024], P('seq', 'chan'), may hold values from -6 to 6
- out_grad: bfloat16 [262144, 1024], P('seq', 'chan'), may hold values from -6 to 6
- kernel: bfloat16 [512, 512, 1024], P('seq', None, 'chan'), may hold values from -4 to 4
- gate_weight: bfloat16 [1024, 1024], P(None, 'chan'), may hold values from -0.1875 to 0.1875
- right_factor: bfloat16 [512, 512], replicated, may hold values from -0.25 to 0.25
- left_factor: bfloat16 [512, 512], replicated, may hold values from -0.25 to 0.25
Outputs:
- input_grad: bfloat16 [262144, 1024], P('seq', 'chan')
- kernel_grad: bfloat16 [512, 512, 1024], P('seq', None, 'chan')
- right_grad: float32 [262144], P(('seq', 'chan'))
- left_grad: float32 [262144], P(('seq', 'chan'))
- gate_weight_grad: float32 [1024, 1024], P(('seq', 'chan'))
All inputs are finite; a program needn't handle non-finite values.
Results may differ from a plain program's by a relative error of at most 0.015.
Values may be sent and summed in bfloat16 or wider, within the bound.
No kernel may reach another device: no remote copies, remote signals or barrier semaphores. Data moves between devices by JAX's collectives and lax.ppermute only.
A program may use at most 128 MiB of HBM per device.

v0:
```python
import jax
import jax.numpy as jnp
from jax import lax
from jax.sharding import PartitionSpec as P


def local(inputs, out_grad, kernel, gate_weight, right_factor, left_factor):
    block = right_factor.shape[0]
    rows, width = inputs.shape
    model_width = gate_weight.shape[0]
    local_blocks = rows // block
    blocks_in = inputs.reshape(local_blocks, block, width)
    first = jnp.einsum(
        "abc,jb->ajc", blocks_in, right_factor, preferred_element_type=jnp.float32
    ).astype(jnp.bfloat16)
    scaled = (first.astype(jnp.float32) * kernel.astype(jnp.float32)).astype(jnp.bfloat16)
    piece = lax.all_to_all(scaled, "seq", split_axis=1, concat_axis=0, tiled=True)
    product = jnp.einsum("ia,ajc->jic", left_factor, piece, preferred_element_type=jnp.float32)
    mixed_cube = product.astype(jnp.bfloat16)
    mixed = mixed_cube.reshape(rows, width)
    full_weight = lax.all_gather(gate_weight, "chan", axis=1, tiled=True)
    rows_in = lax.all_to_all(inputs, "chan", split_axis=0, concat_axis=1, tiled=True)
    pre_tok = jnp.dot(rows_in, full_weight, preferred_element_type=jnp.float32)
    gate_tok = jax.nn.sigmoid(pre_tok).astype(jnp.bfloat16)
    gate = lax.all_to_all(gate_tok, "chan", split_axis=1, concat_axis=0, tiled=True)
    gate_wide = gate.astype(jnp.float32)
    cot_wide = out_grad.astype(jnp.float32)
    grad_mixed = (cot_wide * gate_wide).astype(jnp.bfloat16)
    grad_pre = (cot_wide * mixed.astype(jnp.float32) * gate_wide * (1.0 - gate_wide)).astype(
        jnp.bfloat16
    )
    pre_rows = lax.all_to_all(grad_pre, "chan", split_axis=0, concat_axis=1, tiled=True)
    gate_in_rows = jnp.einsum(
        "nk,dk->nd", pre_rows, full_weight, preferred_element_type=jnp.float32
    ).astype(jnp.bfloat16)
    weight_raw = jnp.einsum("nd,nk->dk", rows_in, pre_rows, preferred_element_type=jnp.float32)
    gate_input_grad = lax.all_to_all(gate_in_rows, "chan", split_axis=1, concat_axis=0, tiled=True)
    grad_cube = grad_mixed.reshape(local_blocks, block, width)
    grad_mid = jnp.einsum(
        "ia,jic->ajc", left_factor, grad_cube, preferred_element_type=jnp.float32
    ).astype(jnp.bfloat16)
    left_raw = jnp.einsum("jic,ajc->ia", grad_cube, piece, preferred_element_type=jnp.float32)
    grad_blocks = lax.all_to_all(grad_mid, "seq", split_axis=0, concat_axis=1, tiled=True)
    grad_wide = grad_blocks.astype(jnp.float32)
    grad_first = (grad_wide * kernel.astype(jnp.float32)).astype(jnp.bfloat16)
    kernel_grad = (grad_wide * first.astype(jnp.float32)).astype(jnp.bfloat16)
    right_raw = jnp.einsum("ajc,abc->jb", grad_first, blocks_in, preferred_element_type=jnp.float32)
    back = jnp.einsum(
        "ajc,jb->abc", grad_first, right_factor, preferred_element_type=jnp.float32
    ).reshape(rows, width)
    input_grad = (back + gate_input_grad.astype(jnp.float32)).astype(jnp.bfloat16)
    right_flat = right_raw.reshape(block * block)
    left_flat = left_raw.reshape(block * block)
    right_share, left_share, weight_share = (
        lax.psum_scatter(right_flat, ("seq", "chan"), scatter_dimension=0, tiled=True),
        lax.psum_scatter(left_flat, ("seq", "chan"), scatter_dimension=0, tiled=True),
        lax.psum_scatter(weight_raw, ("seq", "chan"), scatter_dimension=0, tiled=True),
    )
    factor_scale = 1.0 / jnp.sqrt(jnp.float32(block * model_width))
    token_scale = 1.0 / jnp.sqrt(jnp.float32(block * block))
    return (
        input_grad,
        kernel_grad,
        right_share * factor_scale,
        left_share * factor_scale,
        weight_share * token_scale,
    )


def solution(mesh):
    in_specs = (
        P("seq", "chan"),
        P("seq", "chan"),
        P("seq", None, "chan"),
        P(None, "chan"),
        P(),
        P(),
    )
    out_specs = (
        P("seq", "chan"),
        P("seq", None, "chan"),
        P(("seq", "chan")),
        P(("seq", "chan")),
        P(("seq", "chan"), None),
    )
    return jax.shard_map(local, mesh=mesh, in_specs=in_specs, out_specs=out_specs, check_vma=False)
```

profile of v0, /device:TPU:2, one launch (start us, length us, event | category | flops | bytes accessed | tf_op | source)
XLA Modules:
  0.0 548.6 jit_solution(11313670629219693192)
XLA Ops:
  7.2 6.2 %all-to-all-start = ((bf16[8,1024,128]{2,1,0:T(8,128)(2,1)}), bf16[8,1024,128]{2,1,0:T(8,128)(2,1)}, u32[]{:S(2)}, u32[]{:S(2)}) async-start(bf16[8,1024,128]{2,1,0:T(8,128)(2,1)} %bitcast.87), calls=%async_computation | async-start | bytes 4194304 | tf_op jit(solution)/shard_map/all_to_all | solution.py:22
  14.1 4.2 fusion.5
  21.0 21.7 %all-to-all-done = bf16[8,1024,128]{2,1,0:T(8,128)(2,1)} async-done(((bf16[8,1024,128]{2,1,0:T(8,128)(2,1)}), bf16[8,1024,128]{2,1,0:T(8,128)(2,1)}, u32[]{:S(2)}, u32[]{:S(2)}) %all-to-all-start) | async-done | bytes 2097184 | tf_op jit(solution)/shard_map/all_to_all | solution.py:22
  42.7 10.1 %all-to-all-start.3 = ((bf16[16,512,128]{2,0,1:T(8,128)(2,1)}), bf16[16,512,128]{2,0,1:T(8,128)(2,1)}, u32[]{:S(2)}, u32[]{:S(2)}) async-start(bf16[16,512,128]{2,0,1:T(8,128)(2,1)} %copy.67), calls=%async_computation.3 | async-start | bytes 4194304 | tf_op jit(solution)/shard_map/all_to_all | solution.py:17
  52.8 3.9 copy.60
  56.8 35.6 %all-gather.2.cloned.1.call-done = bf16[1024,1024]{1,0:T(8,128)(2,1)} async-done(((bf16[1024,128]{1,0:T(8,128)(2,1)}), bf16[1024,1024]{1,0:T(8,128)(2,1)}) %all-gather.2.cloned.1.call-update) | async-done | bytes 2097168 | tf_op jit(solution)/shard_map/all_gather | solution.py:21
  92.4 6.5 %divide_convert_fusion = bf16[1024,1024]{0,1:T(8,128)(2,1)} fusion(bf16[1024,1024]{0,1:T(8,128)(2,1)} %bitcast.97, bf16[1024,1024]{1,0:T(8,128)(2,1)} %all-gather.2.cloned.1.call-done), kind=kOutput, calls=%fused_computation.19 | convolution fusion | flops 2151677952 | bytes 6291456 | tf_op jit(solution)/shard_map/dot_general | solution.py:23
  101.9 4.4 all-to-all-start.1
  109.9 3.4 convert_bitcast_fusion.2
  113.2 5.3 copy.71
  118.5 14.5 %all-to-all-done.1 = bf16[1024,8,128]{0,2,1:T(8,128)(2,1)} async-done(((bf16[1024,8,128]{0,2,1:T(8,128)(2,1)}), bf16[1024,8,128]{0,2,1:T(8,128)(2,1)}, u32[]{:S(2)}, u32[]{:S(2)}) %all-to-all-start.1) | async-done | bytes 2097184 | tf_op jit(solution)/shard_map/all_to_all | solution.py:25
  133.1 4.1 convert_bitcast_fusion.3
  137.1 5.4 copy.61
  142.5 7.2 %fusion = (bf16[8192,128]{1,0:T(8,128)(2,1)}, bf16[8192,128]{1,0:T(8,128)(2,1)}) fusion(bf16[8192,128]{1,0:T(8,128)(2,1)} %param.7, f32[8,1024,128]{2,1,0:T(8,128)} %copy.61, f32[16,512,128]{2,1,0:T(8,128)} %copy.71), kind=kLoop, calls=%fused_computation.4 | loop fusion | flops 8388608 | bytes 14680064 | tf_op jit(solution)/shard_map/convert_element_type | solution.py:28
  149.7 4.0 copy.72
  153.7 4.7 all-to-all-start.4
  158.5 4.2 convert_bitcast_fusion.4
  162.7 4.6 copy.63
  167.3 17.9 %all-to-all-done.4 = bf16[8,1024,128]{1,2,0:T(8,128)(2,1)} async-done(((bf16[8,1024,128]{1,2,0:T(8,128)(2,1)}), bf16[8,1024,128]{1,2,0:T(8,128)(2,1)}, u32[]{:S(2)}, u32[]{:S(2)}) %all-to-all-start.4) | async-done | bytes 2097184 | tf_op jit(solution)/shard_map/all_to_all | solution.py:32
  185.2 6.1 %all-to-all-start.2 = ((bf16[512,16,128]{2,1,0:T(8,128)(2,1)}), bf16[512,16,128]{2,1,0:T(8,128)(2,1)}, u32[]{:S(2)}, u32[]{:S(2)}) async-start(bf16[512,16,128]{2,1,0:T(8,128)(2,1)} %copy.63), calls=%async_computation.2 | async-start | bytes 4194304 | tf_op jit(solution)/shard_map/all_to_all | solution.py:43
  191.3 3.5 fusion.11
  196.8 5.3 convolution_convert_fusion
  202.0 38.3 %all-to-all-done.2 = bf16[512,16,128]{2,1,0:T(8,128)(2,1)} async-done(((bf16[512,16,128]{2,1,0:T(8,128)(2,1)}), bf16[512,16,128]{2,1,0:T(8,128)(2,1)}, u32[]{:S(2)}, u32[]{:S(2)}) %all-to-all-start.2) | async-done | bytes 2097184 | tf_op jit(solution)/shard_map/all_to_all | solution.py:43
  240.3 4.8 all-to-all-start.5
  245.2 6.5 %convolution_bitcast_fusion = f32[1024,1024]{0,1:T(8,128)} fusion(bf16[1024,1024]{0,1:T(8,128)(2,1)} %bitcast.25, bf16[1024,1024]{0,1:T(8,128)(2,1)} %bitcast.98), kind=kOutput, calls=%fused_computation.20 | convolution fusion | flops 2147483648 | bytes 8388608 | tf_op jit(solution)/shard_map/nd,nk->dk/dot_general | solution.py:36
  261.3 10.4 %all-to-all-done.5 = bf16[1024,8,128]{0,2,1:T(8,128)(2,1)} async-done(((bf16[1024,8,128]{0,2,1:T(8,128)(2,1)}), bf16[1024,8,128]{0,2,1:T(8,128)(2,1)}, u32[]{:S(2)}, u32[]{:S(2)}) %all-to-all-start.5) | async-done | bytes 2097184 | tf_op jit(solution)/shard_map/all_to_all | solution.py:37
  271.7 4.3 convert_bitcast_fusion.1
  276.0 5.5 %copy.73 = f32[8,1024,128]{2,1,0:T(8,128)} copy(f32[8,1024,128]{1,2,0:T(8,128)} %convert_bitcast_fusion.1) | data formatting | bytes 8388608 | tf_op jit(solution)/shard_map/convert_element_type | solution.py:51
  281.5 3.2 convolution_bitcast_fusion.1
  284.7 5.4 copy.66
  290.1 5.3 fusion.6
  295.4 243.0 %all-reduce.6.cloned.1.call-done = (f32[262144]{0:T(1024)}, f32[262144]{0:T(1024)}, f32[1024,1024]{0,1:T(8,128)}) async-done(((f32[262144]{0:T(1024)}, f32[262144]{0:T(1024)}, f32[1024,1024]{0,1:T(8,128)}), (f32[262144]{0:T(1024)}, f32[262144]{0:T(1024)}, f32[1024,1024]{0,1:T(8,128)})) %all-reduce.6.cloned.1.call-update) | async-done | bytes 6291472
  (34 shorter events, 24.9 us)
Async XLA Ops:
  7.2 6.9 %copy-start = (bf16[512,512]{1,0:T(8,128)(2,1)S(1)}, bf16[512,512]{1,0:T(8,128)(2,1)}, u32[]{:S(2)}) copy-start(bf16[512,512]{1,0:T(8,128)(2,1)} %param.10) | copy-start | bytes 1572868
  7.2 6.9 %copy-start.1 = (bf16[8192,128]{1,0:T(8,128)(2,1)S(1)}, bf16[8192,128]{1,0:T(8,128)(2,1)}, u32[]{:S(2)}) copy-start(bf16[8192,128]{1,0:T(8,128)(2,1)} %param.6) | copy-start | bytes 6291460
  7.2 35.5 %all-to-all-start = ((bf16[8,1024,128]{2,1,0:T(8,128)(2,1)}), bf16[8,1024,128]{2,1,0:T(8,128)(2,1)}, u32[]{:S(2)}, u32[]{:S(2)}) async-start(bf16[8,1024,128]{2,1,0:T(8,128)(2,1)} %bitcast.87), calls=%async_computation | async-start | bytes 4194304 | tf_op jit(solution)/shard_map/all_to_all | solution.py:22
  13.4 79.0 %all-gather.2.cloned.1.call-start = ((), (), s32[]{:S(2)}) async-start(), calls=%async_computation.6 | async-start | bytes 2359296 | tf_op jit(solution)/shard_map/all_gather | solution.py:21
  42.7 59.2 %all-to-all-start.3 = ((bf16[16,512,128]{2,0,1:T(8,128)(2,1)}), bf16[16,512,128]{2,0,1:T(8,128)(2,1)}, u32[]{:S(2)}, u32[]{:S(2)}) async-start(bf16[16,512,128]{2,0,1:T(8,128)(2,1)} %copy.67), calls=%async_computation.3 | async-start | bytes 4194304 | tf_op jit(solution)/shard_map/all_to_all | solution.py:17
  101.9 31.1 %all-to-all-start.1 = ((bf16[1024,8,128]{0,2,1:T(8,128)(2,1)}), bf16[1024,8,128]{0,2,1:T(8,128)(2,1)}, u32[]{:S(2)}, u32[]{:S(2)}) async-start(bf16[1024,8,128]{0,2,1:T(8,128)(2,1)} %bitcast.100), calls=%async_computation.1 | async-start | bytes 4194304 | tf_op jit(solution)/shard_map/all_to_all | solution.py:25
  106.3 3.6 copy-start.7
  108.5 1.4 copy-start.4
  153.7 31.4 %all-to-all-start.4 = ((bf16[8,1024,128]{1,2,0:T(8,128)(2,1)}), bf16[8,1024,128]{1,2,0:T(8,128)(2,1)}, u32[]{:S(2)}, u32[]{:S(2)}) async-start(bf16[8,1024,128]{1,2,0:T(8,128)(2,1)} %copy.72), calls=%async_computation.4 | async-start | bytes 4194304 | tf_op jit(solution)/shard_map/all_to_all | solution.py:32
  185.2 55.2 %all-to-all-start.2 = ((bf16[512,16,128]{2,1,0:T(8,128)(2,1)}), bf16[512,16,128]{2,1,0:T(8,128)(2,1)}, u32[]{:S(2)}, u32[]{:S(2)}) async-start(bf16[512,16,128]{2,1,0:T(8,128)(2,1)} %copy.63), calls=%async_computation.2 | async-start | bytes 4194304 | tf_op jit(solution)/shard_map/all_to_all | solution.py:43
  194.8 2.0 copy-start.8
  240.3 31.3 %all-to-all-start.5 = ((bf16[1024,8,128]{0,2,1:T(8,128)(2,1)}), bf16[1024,8,128]{0,2,1:T(8,128)(2,1)}, u32[]{:S(2)}, u32[]{:S(2)}) async-start(bf16[1024,8,128]{0,2,1:T(8,128)(2,1)} %bitcast.99), calls=%async_computation.5 | async-start | bytes 4194304 | tf_op jit(solution)/shard_map/all_to_all | solution.py:37
  245.1 293.3 %all-reduce.6.cloned.1.call-start = ((), (), s32[]{:S(2)}) async-start(), calls=%async_computation.7 | async-start | bytes 12582912
  253.8 1.6 copy-start.2
  253.8 2.2 copy-start.3
  258.6 1.3 copy-start.5
  276.0 5.5 %copy-start.6 = (bf16[16,512,128]{2,1,0:T(8,128)(2,1)S(1)}, bf16[16,512,128]{2,1,0:T(8,128)(2,1)}, u32[]{:S(2)}) copy-start(bf16[16,512,128]{2,1,0:T(8,128)(2,1)} %copy-done.5) | copy-start | bytes 6291460
Sparse Core Ops, SparseCore 0:
  16.6 75.7 all-gather.1
  261.4 276.9 all-reduce.5
where the time goes:
time: 550 us; the launch traced here: 549 us
  waiting for transfers between devices  385 us (70%)
  local copies, waits for them, and re-layouts  46.7 us (8%)
  matrix products  38.1 us (7%)
  starting transfers between devices  36.4 us (7%)
  other arithmetic  28.1 us (5%)
  between operations  14.2 us (3%)
    unnamed x3, waiting for transfers between devices  244 us
    all_to_all x1, waiting for transfers between devices, local(): lax.all_to_all(grad_mid, 'seq', split_axis=0, concat_axis=1, tiled=True)  38.3 us
    all_gather x1, waiting for transfers between devices, local(): full_weight = lax.all_gather(gate_weight, 'chan', axis=1, tiled=True)  35.6 us
    all_to_all x1, waiting for transfers between devices, local(): lax.all_to_all(inputs, 'chan', split_axis=0, concat_axis=1, tiled=True)  21.7 us
    all_to_all x1, waiting for transfers between devices, local(): lax.all_to_all(grad_pre, 'chan', split_axis=0, concat_axis=1, tiled=True)  17.9 us
    all_to_all x1, waiting for transfers between devices, local(): lax.all_to_all(gate_tok, 'chan', split_axis=1, concat_axis=0, tiled=True)  14.5 us
  transfers between devices with their start and end apart: 8, of which 8 were waited for; matrix products, arithmetic and copies ran while one was open for 16% of the time, Pallas kernels for 0%

commit v1 on v0

--- a/solution.py
+++ b/solution.py
@@ -19,7 +19,10 @@
     mixed_cube = product.astype(jnp.bfloat16)
     mixed = mixed_cube.reshape(rows, width)
     full_weight = lax.all_gather(gate_weight, "chan", axis=1, tiled=True)
-    rows_in = lax.all_to_all(inputs, "chan", split_axis=0, concat_axis=1, tiled=True)
+    rows_in = jnp.concatenate(
+        lax.all_to_all(jnp.stack(jnp.split(inputs, lax.axis_size("chan"), axis=0)), "chan", 0, 0),
+        axis=1,
+    )
     pre_tok = jnp.dot(rows_in, full_weight, preferred_element_type=jnp.float32)
     gate_tok = jax.nn.sigmoid(pre_tok).astype(jnp.bfloat16)
     gate = lax.all_to_all(gate_tok, "chan", split_axis=1, concat_axis=0, tiled=True)

time: 550 us -> 558 us (1.015)
    unnamed x21 -> x35, local copies, waits for them, and re-layouts: 7.27 us -> 12.7 us
  transfers between devices with their start and end apart: 8 -> 8, of which waited for: 8 -> 8; matrix products, arithmetic and copies ran while one was open for 16% -> 15% of each run, Pallas kernels for 0% -> 0%
where the time goes in v1:
time: 558 us; the launch traced here: 557 us
  waiting for transfers between devices  389 us (70%)
  local copies, waits for them, and re-layouts  50.5 us (9%)
  matrix products  38.2 us (7%)
  starting transfers between devices  36.7 us (7%)
  other arithmetic  28.1 us (5%)
  between operations  14.2 us (3%)
    unnamed x3, waiting for transfers between devices  244 us
    all_gather x1, waiting for transfers between devices, local(): full_weight = lax.all_gather(gate_weight, 'chan', axis=1, tiled=True)  39.5 us
    all_to_all x1, waiting for transfers between devices, local(): lax.all_to_all(grad_mid, 'seq', split_axis=0, concat_axis=1, tiled=True)  38.4 us
    all_to_all x1, waiting for transfers between devices, local(): lax.all_to_all(jnp.stack(jnp.split(inputs, lax.axis_size('chan'), axis=0)...  21.7 us
    all_to_all x1, waiting for transfers between devices, local(): lax.all_to_all(grad_pre, 'chan', split_axis=0, concat_axis=1, tiled=True)  17.9 us
    all_to_all x1, waiting for transfers between devices, local(): lax.all_to_all(gate_tok, 'chan', split_axis=1, concat_axis=0, tiled=True)  14.4 us
    unnamed x35, local copies, waits for them, and re-layouts  12.7 us
  transfers between devices with their start and end apart: 8, of which 8 were waited for; matrix products, arithmetic and copies ran while one was open for 15% of the time, Pallas kernels for 0%

profile of v1, /device:TPU:2, one launch (start us, length us, event | category | flops | bytes accessed | tf_op | source)
XLA Modules:
  0.0 556.6 jit_solution(3980552262787834899)
XLA Ops:
  15.9 6.2 %all-to-all-start = ((bf16[8,1024,128]{1,2,0:T(8,128)(2,1)}), bf16[8,1024,128]{1,2,0:T(8,128)(2,1)}, u32[]{:S(2)}, u32[]{:S(2)}) async-start(bf16[8,1024,128]{1,2,0:T(8,128)(2,1)} %bitcast_dynamic-update-slice_fusion), calls=%async_computation | async-start | bytes 4194304 | tf_op jit(solution)/shard_map/all_to_all | solution.py:23
  22.8 4.2 fusion.5
  29.7 21.7 %all-to-all-done = bf16[8,1024,128]{1,2,0:T(8,128)(2,1)} async-done(((bf16[8,1024,128]{1,2,0:T(8,128)(2,1)}), bf16[8,1024,128]{1,2,0:T(8,128)(2,1)}, u32[]{:S(2)}, u32[]{:S(2)}) %all-to-all-start) | async-done | bytes 2097184 | tf_op jit(solution)/shard_map/all_to_all | solution.py:23
  51.4 10.1 %all-to-all-start.3 = ((bf16[16,512,128]{2,0,1:T(8,128)(2,1)}), bf16[16,512,128]{2,0,1:T(8,128)(2,1)}, u32[]{:S(2)}, u32[]{:S(2)}) async-start(bf16[16,512,128]{2,0,1:T(8,128)(2,1)} %copy.72), calls=%async_computation.3 | async-start | bytes 4194304 | tf_op jit(solution)/shard_map/all_to_all | solution.py:17
  61.5 39.5 %all-gather.2.cloned.1.call-done = bf16[1024,1024]{1,0:T(8,128)(2,1)} async-done(((bf16[1024,128]{1,0:T(8,128)(2,1)}), bf16[1024,1024]{1,0:T(8,128)(2,1)}) %all-gather.2.cloned.1.call-update) | async-done | bytes 2097168 | tf_op jit(solution)/shard_map/all_gather | solution.py:21
  101.1 6.5 %divide_convert_fusion = bf16[1024,1024]{0,1:T(8,128)(2,1)} fusion(bf16[1024,1024]{0,1:T(8,128)(2,1)} %bitcast.9, bf16[1024,1024]{1,0:T(8,128)(2,1)} %all-gather.2.cloned.1.call-done), kind=kOutput, calls=%fused_computation.19 | convolution fusion | flops 2151677952 | bytes 6291456 | tf_op jit(solution)/shard_map/dot_general | solution.py:26
  107.6 3.0 all-to-all-done.3
  110.6 4.5 all-to-all-start.1
  118.7 3.4 convert_bitcast_fusion.2
  122.1 5.3 copy.76
  127.4 14.4 %all-to-all-done.1 = bf16[1024,8,128]{0,2,1:T(8,128)(2,1)} async-done(((bf16[1024,8,128]{0,2,1:T(8,128)(2,1)}), bf16[1024,8,128]{0,2,1:T(8,128)(2,1)}, u32[]{:S(2)}, u32[]{:S(2)}) %all-to-all-start.1) | async-done | bytes 2097184 | tf_op jit(solution)/shard_map/all_to_all | solution.py:28
  141.7 4.0 convert_bitcast_fusion.3
  145.8 5.4 copy.66
  151.2 7.2 %fusion = (bf16[8192,128]{1,0:T(8,128)(2,1)}, bf16[8192,128]{1,0:T(8,128)(2,1)}) fusion(bf16[8192,128]{1,0:T(8,128)(2,1)} %param.7, f32[8,1024,128]{2,1,0:T(8,128)} %copy.66, f32[16,512,128]{2,1,0:T(8,128)} %copy.76), kind=kLoop, calls=%fused_computation.4 | loop fusion | flops 8388608 | bytes 14680064 | tf_op jit(solution)/shard_map/convert_element_type | solution.py:31
  158.4 3.9 copy.77
  162.3 4.7 all-to-all-start.4
  167.0 4.3 convert_bitcast_fusion.4
  171.3 4.5 copy.68
  175.8 17.9 %all-to-all-done.4 = bf16[8,1024,128]{1,2,0:T(8,128)(2,1)} async-done(((bf16[8,1024,128]{1,2,0:T(8,128)(2,1)}), bf16[8,1024,128]{1,2,0:T(8,128)(2,1)}, u32[]{:S(2)}, u32[]{:S(2)}) %all-to-all-start.4) | async-done | bytes 2097184 | tf_op jit(solution)/shard_map/all_to_all | solution.py:35
  193.8 6.1 %all-to-all-start.2 = ((bf16[512,16,128]{2,1,0:T(8,128)(2,1)}), bf16[512,16,128]{2,1,0:T(8,128)(2,1)}, u32[]{:S(2)}, u32[]{:S(2)}) async-start(bf16[512,16,128]{2,1,0:T(8,128)(2,1)} %copy.68), calls=%async_computation.2 | async-start | bytes 4194304 | tf_op jit(solution)/shard_map/all_to_all | solution.py:46
  199.9 3.5 fusion.11
  205.4 5.2 convolution_convert_fusion
  210.6 38.4 %all-to-all-done.2 = bf16[512,16,128]{2,1,0:T(8,128)(2,1)} async-done(((bf16[512,16,128]{2,1,0:T(8,128)(2,1)}), bf16[512,16,128]{2,1,0:T(8,128)(2,1)}, u32[]{:S(2)}, u32[]{:S(2)}) %all-to-all-start.2) | async-done | bytes 2097184 | tf_op jit(solution)/shard_map/all_to_all | solution.py:46
  248.9 4.8 all-to-all-start.5
  254.0 6.6 %fusion.19 = f32[1024,1024]{1,0:T(8,128)} fusion(bf16[1024,1024]{0,1:T(8,128)(2,1)} %bitcast.9, bf16[1024,1024]{0,1:T(8,128)(2,1)} %bitcast.32), kind=kOutput, calls=%fused_computation.45 | convolution fusion | flops 2147483648 | bytes 8388608 | tf_op jit(solution)/shard_map/nd,nk->dk/dot_general | solution.py:39
  270.2 10.1 %all-to-all-done.5 = bf16[1024,8,128]{0,2,1:T(8,128)(2,1)} async-done(((bf16[1024,8,128]{0,2,1:T(8,128)(2,1)}), bf16[1024,8,128]{0,2,1:T(8,128)(2,1)}, u32[]{:S(2)}, u32[]{:S(2)}) %all-to-all-start.5) | async-done | bytes 2097184 | tf_op jit(solution)/shard_map/all_to_all | solution.py:40
  280.3 4.2 convert_bitcast_fusion.1
  284.5 5.5 copy.78
  290.1 3.3 convolution_bitcast_fusion
  293.3 5.4 copy.71
  298.7 5.3 fusion.6
  304.0 243.1 %all-reduce.6.cloned.1.call-done = (f32[262144]{0:T(1024)}, f32[262144]{0:T(1024)}, f32[1024,1024]{1,0:T(8,128)}) async-done(((f32[262144]{0:T(1024)}, f32[262144]{0:T(1024)}, f32[1024,1024]{1,0:T(8,128)}), (f32[262144]{0:T(1024)}, f32[262144]{0:T(1024)}, f32[1024,1024]{1,0:T(8,128)})) %all-reduce.6.cloned.1.call-update) | async-done | bytes 6291472
  (49 shorter events, 30.0 us)
Async XLA Ops:
  7.2 15.6 %copy-start = (bf16[512,512]{1,0:T(8,128)(2,1)S(1)}, bf16[512,512]{1,0:T(8,128)(2,1)}, u32[]{:S(2)}) copy-start(bf16[512,512]{1,0:T(8,128)(2,1)} %param.10) | copy-start | bytes 1572868
  15.9 6.9 %copy-start.1 = (bf16[8192,128]{1,0:T(8,128)(2,1)S(1)}, bf16[8192,128]{1,0:T(8,128)(2,1)}, u32[]{:S(2)}) copy-start(bf16[8192,128]{1,0:T(8,128)(2,1)} %param.6) | copy-start | bytes 6291460
  15.9 35.5 %all-to-all-start = ((bf16[8,1024,128]{1,2,0:T(8,128)(2,1)}), bf16[8,1024,128]{1,2,0:T(8,128)(2,1)}, u32[]{:S(2)}, u32[]{:S(2)}) async-start(bf16[8,1024,128]{1,2,0:T(8,128)(2,1)} %bitcast_dynamic-update-slice_fusion), calls=%async_computation | async-start | bytes 4194304 | tf_op jit(solution)/shard_map/all_to_all | solution.py:23
  22.0 79.0 %all-gather.2.cloned.1.call-start = ((), (), s32[]{:S(2)}) async-start(), calls=%async_computation.6 | async-start | bytes 2359296 | tf_op jit(solution)/shard_map/all_gather | solution.py:21
  51.4 59.2 %all-to-all-start.3 = ((bf16[16,512,128]{2,0,1:T(8,128)(2,1)}), bf16[16,512,128]{2,0,1:T(8,128)(2,1)}, u32[]{:S(2)}, u32[]{:S(2)}) async-start(bf16[16,512,128]{2,0,1:T(8,128)(2,1)} %copy.72), calls=%async_computation.3 | async-start | bytes 4194304 | tf_op jit(solution)/shard_map/all_to_all | solution.py:17
  110.6 31.1 %all-to-all-start.1 = ((bf16[1024,8,128]{0,2,1:T(8,128)(2,1)}), bf16[1024,8,128]{0,2,1:T(8,128)(2,1)}, u32[]{:S(2)}, u32[]{:S(2)}) async-start(bf16[1024,8,128]{0,2,1:T(8,128)(2,1)} %bitcast.109), calls=%async_computation.1 | async-start | bytes 4194304 | tf_op jit(solution)/shard_map/all_to_all | solution.py:28
  115.2 3.6 copy-start.7
  117.4 1.3 copy-start.4
  162.3 31.4 %all-to-all-start.4 = ((bf16[8,1024,128]{1,2,0:T(8,128)(2,1)}), bf16[8,1024,128]{1,2,0:T(8,128)(2,1)}, u32[]{:S(2)}, u32[]{:S(2)}) async-start(bf16[8,1024,128]{1,2,0:T(8,128)(2,1)} %copy.77), calls=%async_computation.4 | async-start | bytes 4194304 | tf_op jit(solution)/shard_map/all_to_all | solution.py:35
  193.8 55.2 %all-to-all-start.2 = ((bf16[512,16,128]{2,1,0:T(8,128)(2,1)}), bf16[512,16,128]{2,1,0:T(8,128)(2,1)}, u32[]{:S(2)}, u32[]{:S(2)}) async-start(bf16[512,16,128]{2,1,0:T(8,128)(2,1)} %copy.68), calls=%async_computation.2 | async-start | bytes 4194304 | tf_op jit(solution)/shard_map/all_to_all | solution.py:46
  203.4 2.0 copy-start.8
  248.9 31.3 %all-to-all-start.5 = ((bf16[1024,8,128]{0,2,1:T(8,128)(2,1)}), bf16[1024,8,128]{0,2,1:T(8,128)(2,1)}, u32[]{:S(2)}, u32[]{:S(2)}) async-start(bf16[1024,8,128]{0,2,1:T(8,128)(2,1)} %bitcast.108), calls=%async_computation.5 | async-start | bytes 4194304 | tf_op jit(solution)/shard_map/all_to_all | solution.py:40
  253.7 293.4 %all-reduce.6.cloned.1.call-start = ((), (), s32[]{:S(2)}) async-start(), calls=%async_computation.7 | async-start | bytes 12582912
  262.6 1.6 copy-start.2
  262.7 2.2 copy-start.3
  267.5 1.3 copy-start.5
  284.5 5.5 copy-start.6
Sparse Core Ops, SparseCore 0:
  25.3 75.7 all-gather.1
  270.3 276.7 all-reduce.5
